TPU v7x, 256 devices: a whole 4x4x8 slice. The times are simulated.
256 devices in a mesh: gx: 16 (over x, z_hi), gy: 8 (over y, core), ga: 2 (over z_lo).
Axes of the slice: x: 4, y: 4, z: 8 (z_hi: 4, z_lo: 2; z = z_hi * 2 + z_lo), core: 2. Of those that a mesh axis runs over, the one named last changes fastest.
Arguments:
- head: float32 [16, 256, 8192], P(None, 'gx', ('gy', 'ga')), may hold values from -6 to 6
- conductivity: float32 [16, 256, 8192], P(None, 'gx', ('gy', 'ga')), may hold values from 0.1 to 10
- root_layer: int32 [256, 8192], P('gx', ('gy', 'ga')), may hold values from 0 to 15
- veg_type: int32 [256, 8192], P('gx', ('gy', 'ga')), may hold values from 0 to 16
- uptake_rate: float32 [17], replicated, may hold values from 0.2 to 2
- depth: float32 [256, 8192], P('gx'), may hold values from 0.05 to 2
- conveyance: float32 [256, 8192], P('gx'), may hold values from 0.2 to 5
- elevation: float32 [256, 8192], P('gx'), may hold values from -3 to 3
- land_mask: int32 [256, 8192], P('gx'), may hold values 0 or 1
Outputs:
- new_head: float32 [16, 256, 8192], P(None, 'gx', ('gy', 'ga'))
- new_depth: float32 [256, 8192], P('gx')
All inputs are finite; a program needn't handle non-finite values. No bound on the sum of `land_mask` on one device may be relied on, other than what follows from the above.
Results may differ from a plain program's by a relative error of at most 0.0003.
Values sent between devices are 32-bit elements; how exact they have to be, the bound alone decides.
A program may use at most 64 MiB of HBM per device.

v0:
```python
import jax
import jax.numpy as jnp
from jax import lax
from jax.sharding import PartitionSpec as P

NVEG = 17
SSW = 4
exchange_coef = 0.5
storage_coef = 0.5


def with_halo(cells, sides, width):
    for axis, dim in sides:
        count = lax.axis_size(axis)
        ends = count - 1
        head = lax.slice_in_dim(cells, 0, width, axis=dim)
        tail = lax.slice_in_dim(cells, cells.shape[dim] - width, cells.shape[dim], axis=dim)
        cells = jnp.concatenate(
            [
                lax.ppermute(tail, axis, [(i, (i + 1) % count) for i in range(ends)]),
                cells,
                lax.ppermute(head, axis, [((i + 1) % count, i) for i in range(ends)]),
            ],
            axis=dim,
        )
    return cells


def harmonic(first, second):
    total = first + second
    return 2.0 * first * second / jnp.where(total > 0, total, 1.0)


def lateral(field_ext, coef_ext):
    center = coef_ext[..., 1:-1, 1:-1]
    wsum = jnp.zeros_like(center)
    nsum = jnp.zeros_like(center)
    for rows, cols in (
        (slice(2, None), slice(1, -1)),
        (slice(None, -2), slice(1, -1)),
        (slice(1, -1), slice(2, None)),
        (slice(1, -1), slice(None, -2)),
    ):
        weight = harmonic(center, coef_ext[..., rows, cols])
        wsum = wsum + weight
        nsum = nsum + weight * field_ext[..., rows, cols]
    return (wsum, nsum)


def guarded(numer, denom):
    return jnp.where(denom > 0, numer / jnp.where(denom > 0, denom, 1.0), 0.0)


def surface_sweep(depth_ext, drag_ext, bed_ext, base, diag):
    wsum, nsum = lateral(depth_ext + bed_ext, drag_ext)
    bed = bed_ext[1:-1, 1:-1]
    return guarded(base + nsum - wsum * bed, diag + wsum)


def soil_sweep(head_ext, cond_ext, base, diag):
    cond = cond_ext[:, 1:-1, 1:-1]
    inner = head_ext[:, 1:-1, 1:-1]
    wsum, nsum = lateral(head_ext, cond_ext)
    vertical = harmonic(cond[:-1], cond[1:])
    blank = jnp.zeros_like(cond[:1])
    down = jnp.concatenate([vertical, blank], axis=0)
    upward = jnp.concatenate([blank, vertical], axis=0)
    below = jnp.concatenate([inner[1:], blank], axis=0)
    above = jnp.concatenate([blank, inner[:-1]], axis=0)
    numer = base + nsum + down * (below - 1.0) + upward * (above + 1.0)
    return guarded(numer, diag + wsum + down + upward)


def widen_cols(stacked, width):
    pads = [(0, 0)] * (stacked.ndim - 1) + [(width, width)]
    return jnp.pad(stacked, pads)


def body(
    head, conductivity, root_layer, veg_type, uptake_rate, depth, conveyance, elevation, land_mask
):
    layers_here, rows_here, cols_here = head.shape
    offset = lax.axis_index(("gy", "ga")) * cols_here
    coupling_rows = exchange_coef * land_mask.astype(jnp.float32)
    coupling = lax.dynamic_slice_in_dim(coupling_rows, offset, cols_here, 1)
    top = head[0]
    top_rows = lax.all_gather(top, ("gy", "ga"), axis=1, tiled=True)
    drag = conveyance * jnp.power(depth, 5.0 / 3.0)
    sbase = depth + coupling_rows * top_rows
    sdiag = 1.0 + coupling_rows
    opened = with_halo(jnp.stack([depth, drag, elevation]), (("gx", 1),), 1)
    opened = widen_cols(opened, 1)
    drag_ext = opened[1]
    bed_ext = opened[2]
    level = surface_sweep(opened[0], drag_ext, bed_ext, sbase, sdiag)
    for sweep in range(SSW - 1):
        level_ext = widen_cols(with_halo(level, (("gx", 0),), 1), 1)
        level = surface_sweep(level_ext, drag_ext, bed_ext, sbase, sdiag)
    level_here = lax.dynamic_slice_in_dim(level, offset, cols_here, 1)
    kinds = jnp.arange(NVEG, dtype=jnp.int32)[:, None, None]
    rate = jnp.sum(jnp.where(veg_type[None] == kinds, uptake_rate[:, None, None], 0.0), axis=0)
    layers = jnp.arange(layers_here, dtype=jnp.int32)[:, None, None]
    inside = (layers <= root_layer[None]).astype(jnp.float32)
    sink = rate[None] * inside / (root_layer[None].astype(jnp.float32) + 1.0)
    base = storage_coef * head - sink
    base = base.at[0].add(coupling * level_here)
    diag = jnp.full(head.shape, storage_coef, jnp.float32)
    diag = diag.at[0].add(coupling)
    opened = with_halo(jnp.stack([head, conductivity]), (("gx", 2), (("gy", "ga"), 3)), 1)
    cond_ext = opened[1]
    current = soil_sweep(opened[0], cond_ext, base, diag)
    head_ext = with_halo(current, (("gx", 1), (("gy", "ga"), 2)), 1)
    current = soil_sweep(head_ext, cond_ext, base, diag)
    return (current, level)


def solution(mesh):
    return jax.shard_map(
        body,
        mesh=mesh,
        in_specs=(
            P(None, "gx", ("gy", "ga")),
            P(None, "gx", ("gy", "ga")),
            P("gx", ("gy", "ga")),
            P("gx", ("gy", "ga")),
            P(),
            P("gx", None),
            P("gx", None),
            P("gx", None),
            P("gx", None),
        ),
        out_specs=(P(None, "gx", ("gy", "ga")), P("gx", None)),
        check_vma=False,
    )
```

profile of v0, /device:TPU:34, one launch (start us, length us, event | category | flops | bytes accessed | tf_op | source)
XLA Modules:
  0.0 151.8 jit_solution(12704075630938351134)
XLA Ops:
  2.2 2.0 %pad_maximum_fusion.18 = (f32[3,1,8192]{2,1,0:T(1,128)}, f32[3,1,8192]{2,1,0:T(1,128)}) fusion(f32[1,16,8192]{2,1,0:T(8,128)} %bitcast.50, f32[1,16,8192]{2,1,0:T(8,128)S(1)} %multiply_bitcast_fusion, f32[1,16,8192]{2,1,0:T(8,128)} %bitcast.42), kind=kLoop, calls=%fused_computation.144 | loop fusion | flops 98304 | bytes 1769472 | tf_op jit(solution)/shard_map/slice | solution.py:17
  4.2 5.2 %collective-permute-start.4 = (f32[3,1,8192]{2,1,0:T(1,128)}, f32[3,1,8192]{2,1,0:T(1,128)}, u32[]{:S(2)}, u32[]{:S(2)}) collective-permute-start(f32[3,1,8192]{2,1,0:T(1,128)} %get-tuple-element.35), channel_id=1, source_target_pairs={{0,16},{16,32},{32,48},{48,64},{64,80},{80,96},{96,112},{112,128},... | collective-permute-start | bytes 294920 | tf_op jit(solution)/shard_map/ppermute | solution.py:20
  9.4 4.0 %collective-permute-start.5 = (f32[3,1,8192]{2,1,0:T(1,128)}, f32[3,1,8192]{2,1,0:T(1,128)}, u32[]{:S(2)}, u32[]{:S(2)}) collective-permute-start(f32[3,1,8192]{2,1,0:T(1,128)} %get-tuple-element.36), channel_id=1, source_target_pairs={{16,0},{32,16},{48,32},{64,48},{80,64},{96,80},{112,96},{128,112},... | collective-permute-start | bytes 294920 | tf_op jit(solution)/shard_map/ppermute | solution.py:22
  13.6 3.4 %collective-permute-start = (f32[2,16,1,512]{3,2,1,0:T(1,128)S(1)}, f32[2,16,1,512]{3,2,1,0:T(1,128)S(1)}, u32[]{:S(2)}, u32[]{:S(2)}) collective-permute-start(f32[2,16,1,512]{3,2,1,0:T(1,128)S(1)} %get-tuple-element.39), channel_id=1, source_target_pairs={{0,16},{16,32},{32,48},{48,64},{64,80},{80,96},{96,112},{112,128},... | collective-permute-start | bytes 196616 | tf_op jit(solution)/shard_map/ppermute | solution.py:20
  17.0 5.5 %collective-permute-start.1 = (f32[2,16,1,512]{3,2,1,0:T(1,128)S(1)}, f32[2,16,1,512]{3,2,1,0:T(1,128)S(1)}, u32[]{:S(2)}, u32[]{:S(2)}) collective-permute-start(f32[2,16,1,512]{3,2,1,0:T(1,128)S(1)} %get-tuple-element.40), channel_id=1, source_target_pairs={{16,0},{32,16},{48,32},{64,48},{80,64},{96,80},{112,96},{128,112},... | collective-permute-start | bytes 196616 | tf_op jit(solution)/shard_map/ppermute | solution.py:22
  22.8 2.6 %collective-permute-done.1 = f32[2,16,1,512]{3,2,1,0:T(1,128)S(1)} collective-permute-done((f32[2,16,1,512]{3,2,1,0:T(1,128)S(1)}, f32[2,16,1,512]{3,2,1,0:T(1,128)S(1)}, u32[]{:S(2)}, u32[]{:S(2)}) %collective-permute-start.1) | collective-permute-done | bytes 65568 | tf_op jit(solution)/shard_map/ppermute | solution.py:22
  25.6 1.9 %collective-permute-start.2 = (f32[2,16,18,1]{3,2,1,0:T(8,128)S(1)}, f32[2,16,18,1]{3,2,1,0:T(8,128)}, u32[]{:S(2)}, u32[]{:S(2)}) collective-permute-start(f32[2,16,18,1]{3,2,1,0:T(8,128)S(1)} %get-tuple-element.37), channel_id=1, source_target_pairs={{0,1},{1,2},{2,3},{3,4},{4,5},{5,6},{6,7},{7,8},{8,9},{9,10},{10,1... | collective-permute-start | bytes 6920 | tf_op jit(solution)/shard_map/ppermute | solution.py:20
  27.5 4.7 %collective-permute-start.3 = (f32[2,16,18,1]{3,2,1,0:T(8,128)S(1)}, f32[2,16,18,1]{3,2,1,0:T(8,128)}, u32[]{:S(2)}, u32[]{:S(2)}) collective-permute-start(f32[2,16,18,1]{3,2,1,0:T(8,128)S(1)} %get-tuple-element.38), channel_id=1, source_target_pairs={{1,0},{2,1},{3,2},{4,3},{5,4},{6,5},{7,6},{8,7},{9,8},{10,9},{11,1... | collective-permute-start | bytes 6920 | tf_op jit(solution)/shard_map/ppermute | solution.py:22
  32.2 41.6 %all-gather = f32[1,16,8192]{2,1,0:T(8,128)S(1)} all-gather(f32[1,16,512]{2,1,0:T(8,128)S(1)} %slice.287), channel_id=2, replica_groups=mesh['gx'=16,'gy'=8,'ga'=2] {'gy','ga'}, dimensions={2}, use_global_device_ids=true | all-gather | bytes 557056 | tf_op jit(solution)/shard_map/all_gather | solution.py:87
  73.8 2.3 %pad_maximum_fusion = f32[2,16,18,514]{3,2,1,0:T(8,128)S(1)} fusion(f32[2,16,18,1]{3,2,1,0:T(8,128)} %collective-permute-done.3, f32[2,16,1,512]{3,2,1,0:T(1,128)S(1)} %collective-permute-done.1, f32[1,16,16,512]{3,2,1,0:T(8,128)S(1)} %bitcast.49, f32[1,16,16,512]{3,2,1,0:T(8,128)S(1)} %bitcast.46, f32[2,16,1,512]{3,2,1,0:T(1,128)S(1)} %collective-permute-done, ...), kind=kLoop, calls=%fused_computation.7 | loop fusion | flops 1480320 | bytes 2368512 | tf_op jit(solution)/shard_map/concatenate | solution.py:18
  77.3 2.0 %select_maximum_fusion = f32[3,18,8194]{2,1,0:T(8,128)S(1)} fusion(f32[3,1,8192]{2,1,0:T(1,128)} %collective-permute-done.5, f32[3,1,8192]{2,1,0:T(1,128)} %collective-permute-done.4, f32[1,16,8192]{2,1,0:T(8,128)S(1)} %bitcast.51, f32[1,16,8192]{2,1,0:T(8,128)S(1)} %multiply_bitcast_fusion, f32[1,16,8192]{2,1,0:T(8,128)S(1)} %bitcast.43), kind=kLoop, calls=%fused_computation.2 | loop fusion | flops 5309712 | bytes 3539376 | tf_op jit(solution)/shard_map/concatenate | solution.py:18
  81.8 7.0 %collective-permute-start.6 = (f32[1,8192]{1,0:T(1,128)S(1)}, f32[1,8192]{1,0:T(1,128)S(1)}, u32[]{:S(2)}, u32[]{:S(2)}) collective-permute-start(f32[1,8192]{1,0:T(1,128)S(1)} %get-tuple-element.54), channel_id=1, source_target_pairs={{0,16},{16,32},{32,48},{48,64},{64,80},{80,96},{96,112},{112,128},... | collective-permute-start | bytes 98312 | tf_op jit(solution)/shard_map/ppermute | solution.py:20
  88.7 1.9 %collective-permute-start.7 = (f32[1,8192]{1,0:T(1,128)S(1)}, f32[1,8192]{1,0:T(1,128)S(1)}, u32[]{:S(2)}, u32[]{:S(2)}) collective-permute-start(f32[1,8192]{1,0:T(1,128)S(1)} %get-tuple-element.55), channel_id=1, source_target_pairs={{16,0},{32,16},{48,32},{64,48},{80,64},{96,80},{112,96},{128,112},... | collective-permute-start | bytes 98312 | tf_op jit(solution)/shard_map/ppermute | solution.py:22
  91.0 4.4 %collective-permute-done.7 = f32[1,8192]{1,0:T(1,128)S(1)} collective-permute-done((f32[1,8192]{1,0:T(1,128)S(1)}, f32[1,8192]{1,0:T(1,128)S(1)}, u32[]{:S(2)}, u32[]{:S(2)}) %collective-permute-start.7) | collective-permute-done | bytes 32800 | tf_op jit(solution)/shard_map/ppermute | solution.py:22
  96.7 3.1 %collective-permute-start.8 = (f32[1,8192]{1,0:T(1,128)S(1)}, f32[1,8192]{1,0:T(1,128)S(1)}, u32[]{:S(2)}, u32[]{:S(2)}) collective-permute-start(f32[1,8192]{1,0:T(1,128)S(1)} %get-tuple-element.52), channel_id=1, source_target_pairs={{0,16},{16,32},{32,48},{48,64},{64,80},{80,96},{96,112},{112,128},... | collective-permute-start | bytes 98312 | tf_op jit(solution)/shard_map/ppermute | solution.py:20
  99.9 5.7 %collective-permute-start.9 = (f32[1,8192]{1,0:T(1,128)S(1)}, f32[1,8192]{1,0:T(1,128)S(1)}, u32[]{:S(2)}, u32[]{:S(2)}) collective-permute-start(f32[1,8192]{1,0:T(1,128)S(1)} %get-tuple-element.53), channel_id=1, source_target_pairs={{16,0},{32,16},{48,32},{64,48},{80,64},{96,80},{112,96},{128,112},... | collective-permute-start | bytes 98312 | tf_op jit(solution)/shard_map/ppermute | solution.py:22
  108.4 4.1 %collective-permute-start.10 = (f32[1,8192]{1,0:T(1,128)S(1)}, f32[1,8192]{1,0:T(1,128)S(1)}, u32[]{:S(2)}, u32[]{:S(2)}) collective-permute-start(f32[1,8192]{1,0:T(1,128)S(1)} %get-tuple-element.50), channel_id=1, source_target_pairs={{0,16},{16,32},{32,48},{48,64},{64,80},{80,96},{96,112},{112,128},... | collective-permute-start | bytes 98312 | tf_op jit(solution)/shard_map/ppermute | solution.py:20
  112.5 5.1 %collective-permute-start.11 = (f32[1,8192]{1,0:T(1,128)S(1)}, f32[1,8192]{1,0:T(1,128)S(1)}, u32[]{:S(2)}, u32[]{:S(2)}) collective-permute-start(f32[1,8192]{1,0:T(1,128)S(1)} %get-tuple-element.51), channel_id=1, source_target_pairs={{16,0},{32,16},{48,32},{64,48},{80,64},{96,80},{112,96},{128,112},... | collective-permute-start | bytes 98312 | tf_op jit(solution)/shard_map/ppermute | solution.py:22
  121.9 7.2 %collective-permute-start.12 = (f32[16,1,512]{2,1,0:T(1,128)S(1)}, f32[16,1,512]{2,1,0:T(1,128)S(1)}, u32[]{:S(2)}, u32[]{:S(2)}) collective-permute-start(f32[16,1,512]{2,1,0:T(1,128)S(1)} %get-tuple-element.48), channel_id=1, source_target_pairs={{16,0},{32,16},{48,32},{64,48},{80,64},{96,80},{112,96},{128,112},... | collective-permute-start | bytes 98312 | tf_op jit(solution)/shard_map/ppermute | solution.py:22
  131.1 7.0 %collective-permute-done.13 = f32[16,1,512]{2,1,0:T(1,128)S(1)} collective-permute-done((f32[16,1,512]{2,1,0:T(1,128)S(1)}, f32[16,1,512]{2,1,0:T(1,128)S(1)}, u32[]{:S(2)}, u32[]{:S(2)}) %collective-permute-start.13) | collective-permute-done | bytes 32800 | tf_op jit(solution)/shard_map/ppermute | solution.py:20
  138.3 1.9 %collective-permute-start.14 = (f32[16,18,1]{2,1,0:T(8,128)S(1)}, f32[16,18,1]{2,1,0:T(8,128)S(1)}, u32[]{:S(2)}, u32[]{:S(2)}) collective-permute-start(f32[16,18,1]{2,1,0:T(8,128)S(1)} %get-tuple-element.43), channel_id=1, source_target_pairs={{1,0},{2,1},{3,2},{4,3},{5,4},{6,5},{7,6},{8,7},{9,8},{10,9},{11,1... | collective-permute-start | bytes 3464 | tf_op jit(solution)/shard_map/ppermute | solution.py:22
  140.2 3.6 %collective-permute-start.15 = (f32[16,18,1]{2,1,0:T(8,128)S(1)}, f32[16,18,1]{2,1,0:T(8,128)S(1)}, u32[]{:S(2)}, u32[]{:S(2)}) collective-permute-start(f32[16,18,1]{2,1,0:T(8,128)S(1)} %get-tuple-element.44), channel_id=1, source_target_pairs={{0,1},{1,2},{2,3},{3,4},{4,5},{5,6},{6,7},{7,8},{8,9},{9,10},{10,1... | collective-permute-start | bytes 3464 | tf_op jit(solution)/shard_map/ppermute | solution.py:20
  145.3 4.2 %collective-permute-done.15 = f32[16,18,1]{2,1,0:T(8,128)S(1)} collective-permute-done((f32[16,18,1]{2,1,0:T(8,128)S(1)}, f32[16,18,1]{2,1,0:T(8,128)S(1)}, u32[]{:S(2)}, u32[]{:S(2)}) %collective-permute-start.15) | collective-permute-done | bytes 1184 | tf_op jit(solution)/shard_map/ppermute | solution.py:20
  149.5 2.3 %fusion.20 = f32[16,16,512]{2,1,0:T(8,128)} fusion(f32[16,16,512]{2,1,0:T(8,128)S(1)} %fusion.64, f32[16,18,1]{2,1,0:T(8,128)S(1)} %collective-permute-done.15, f32[16,1,512]{2,1,0:T(1,128)S(1)} %collective-permute-done.12, f32[16,16,512]{2,1,0:T(8,128)S(1)} %fusion.31, f32[16,1,512]{2,1,0:T(1,128)S(1)} %collective-permute-done.13, ...), kind=kLoop, calls=%fused_computation.52 | loop fusion | flops 6946816 | bytes 5769472 | tf_op jit(solution)/shard_map/jit(_where)/select_n | solution.py:51
  (59 shorter events, 17.9 us)
Async XLA Ops:
  0.6 12.8 %copy-start.1 = (f32[16,16,512]{2,1,0:T(8,128)S(1)}, f32[16,16,512]{2,1,0:T(8,128)}, u32[]{:S(2)}) copy-start(f32[16,16,512]{2,1,0:T(8,128)} %param.13) | copy-start | bytes 1572868
  0.6 12.8 %copy-start.3 = (f32[16,16,512]{2,1,0:T(8,128)S(1)}, f32[16,16,512]{2,1,0:T(8,128)}, u32[]{:S(2)}) copy-start(f32[16,16,512]{2,1,0:T(8,128)} %param.14) | copy-start | bytes 1572868
  0.7 21.8 %copy-start.6 = (s32[16,512]{1,0:T(8,128)S(1)}, s32[16,512]{1,0:T(8,128)}, u32[]{:S(2)}) copy-start(s32[16,512]{1,0:T(8,128)} %param.15) | copy-start | bytes 98308
  0.7 21.8 %copy-start.7 = (s32[16,512]{1,0:T(8,128)S(1)}, s32[16,512]{1,0:T(8,128)}, u32[]{:S(2)}) copy-start(s32[16,512]{1,0:T(8,128)} %param.16) | copy-start | bytes 98308
  0.7 21.8 %copy-start.8 = (f32[17]{0:T(128)S(1)}, f32[17]{0:T(128)}, u32[]{:S(2)}) copy-start(f32[17]{0:T(128)} %param.17) | copy-start | bytes 208
  4.2 72.0 %collective-permute-start.4 = (f32[3,1,8192]{2,1,0:T(1,128)}, f32[3,1,8192]{2,1,0:T(1,128)}, u32[]{:S(2)}, u32[]{:S(2)}) collective-permute-start(f32[3,1,8192]{2,1,0:T(1,128)} %get-tuple-element.35), channel_id=1, source_target_pairs={{0,16},{16,32},{32,48},{48,64},{64,80},{80,96},{96,112},{112,128},... | collective-permute-start | bytes 294920 | tf_op jit(solution)/shard_map/ppermute | solution.py:20
  9.4 66.9 %collective-permute-start.5 = (f32[3,1,8192]{2,1,0:T(1,128)}, f32[3,1,8192]{2,1,0:T(1,128)}, u32[]{:S(2)}, u32[]{:S(2)}) collective-permute-start(f32[3,1,8192]{2,1,0:T(1,128)} %get-tuple-element.36), channel_id=1, source_target_pairs={{16,0},{32,16},{48,32},{64,48},{80,64},{96,80},{112,96},{128,112},... | collective-permute-start | bytes 294920 | tf_op jit(solution)/shard_map/ppermute | solution.py:22
  13.6 9.2 %collective-permute-start = (f32[2,16,1,512]{3,2,1,0:T(1,128)S(1)}, f32[2,16,1,512]{3,2,1,0:T(1,128)S(1)}, u32[]{:S(2)}, u32[]{:S(2)}) collective-permute-start(f32[2,16,1,512]{3,2,1,0:T(1,128)S(1)} %get-tuple-element.39), channel_id=1, source_target_pairs={{0,16},{16,32},{32,48},{48,64},{64,80},{80,96},{96,112},{112,128},... | collective-permute-start | bytes 196616 | tf_op jit(solution)/shard_map/ppermute | solution.py:20
  17.0 8.4 %collective-permute-start.1 = (f32[2,16,1,512]{3,2,1,0:T(1,128)S(1)}, f32[2,16,1,512]{3,2,1,0:T(1,128)S(1)}, u32[]{:S(2)}, u32[]{:S(2)}) collective-permute-start(f32[2,16,1,512]{3,2,1,0:T(1,128)S(1)} %get-tuple-element.40), channel_id=1, source_target_pairs={{16,0},{32,16},{48,32},{64,48},{80,64},{96,80},{112,96},{128,112},... | collective-permute-start | bytes 196616 | tf_op jit(solution)/shard_map/ppermute | solution.py:22
  25.6 48.2 %collective-permute-start.2 = (f32[2,16,18,1]{3,2,1,0:T(8,128)S(1)}, f32[2,16,18,1]{3,2,1,0:T(8,128)}, u32[]{:S(2)}, u32[]{:S(2)}) collective-permute-start(f32[2,16,18,1]{3,2,1,0:T(8,128)S(1)} %get-tuple-element.37), channel_id=1, source_target_pairs={{0,1},{1,2},{2,3},{3,4},{4,5},{5,6},{6,7},{7,8},{8,9},{9,10},{10,1... | collective-permute-start | bytes 6920 | tf_op jit(solution)/shard_map/ppermute | solution.py:20
  27.5 46.3 %collective-permute-start.3 = (f32[2,16,18,1]{3,2,1,0:T(8,128)S(1)}, f32[2,16,18,1]{3,2,1,0:T(8,128)}, u32[]{:S(2)}, u32[]{:S(2)}) collective-permute-start(f32[2,16,18,1]{3,2,1,0:T(8,128)S(1)} %get-tuple-element.38), channel_id=1, source_target_pairs={{1,0},{2,1},{3,2},{4,3},{5,4},{6,5},{7,6},{8,7},{9,8},{10,9},{11,1... | collective-permute-start | bytes 6920 | tf_op jit(solution)/shard_map/ppermute | solution.py:22
  76.1 1.0 copy-start
  76.1 1.2 copy-start.4
  81.8 9.2 %collective-permute-start.6 = (f32[1,8192]{1,0:T(1,128)S(1)}, f32[1,8192]{1,0:T(1,128)S(1)}, u32[]{:S(2)}, u32[]{:S(2)}) collective-permute-start(f32[1,8192]{1,0:T(1,128)S(1)} %get-tuple-element.54), channel_id=1, source_target_pairs={{0,16},{16,32},{32,48},{48,64},{64,80},{80,96},{96,112},{112,128},... | collective-permute-start | bytes 98312 | tf_op jit(solution)/shard_map/ppermute | solution.py:20
  88.7 6.7 %collective-permute-start.7 = (f32[1,8192]{1,0:T(1,128)S(1)}, f32[1,8192]{1,0:T(1,128)S(1)}, u32[]{:S(2)}, u32[]{:S(2)}) collective-permute-start(f32[1,8192]{1,0:T(1,128)S(1)} %get-tuple-element.55), channel_id=1, source_target_pairs={{16,0},{32,16},{48,32},{64,48},{80,64},{96,80},{112,96},{128,112},... | collective-permute-start | bytes 98312 | tf_op jit(solution)/shard_map/ppermute | solution.py:22
  96.7 9.2 %collective-permute-start.8 = (f32[1,8192]{1,0:T(1,128)S(1)}, f32[1,8192]{1,0:T(1,128)S(1)}, u32[]{:S(2)}, u32[]{:S(2)}) collective-permute-start(f32[1,8192]{1,0:T(1,128)S(1)} %get-tuple-element.52), channel_id=1, source_target_pairs={{0,16},{16,32},{32,48},{48,64},{64,80},{80,96},{96,112},{112,128},... | collective-permute-start | bytes 98312 | tf_op jit(solution)/shard_map/ppermute | solution.py:20
  99.9 7.3 %collective-permute-start.9 = (f32[1,8192]{1,0:T(1,128)S(1)}, f32[1,8192]{1,0:T(1,128)S(1)}, u32[]{:S(2)}, u32[]{:S(2)}) collective-permute-start(f32[1,8192]{1,0:T(1,128)S(1)} %get-tuple-element.53), channel_id=1, source_target_pairs={{16,0},{32,16},{48,32},{64,48},{80,64},{96,80},{112,96},{128,112},... | collective-permute-start | bytes 98312 | tf_op jit(solution)/shard_map/ppermute | solution.py:22
  108.4 9.2 %collective-permute-start.10 = (f32[1,8192]{1,0:T(1,128)S(1)}, f32[1,8192]{1,0:T(1,128)S(1)}, u32[]{:S(2)}, u32[]{:S(2)}) collective-permute-start(f32[1,8192]{1,0:T(1,128)S(1)} %get-tuple-element.50), channel_id=1, source_target_pairs={{0,16},{16,32},{32,48},{48,64},{64,80},{80,96},{96,112},{112,128},... | collective-permute-start | bytes 98312 | tf_op jit(solution)/shard_map/ppermute | solution.py:20
  112.5 6.7 %collective-permute-start.11 = (f32[1,8192]{1,0:T(1,128)S(1)}, f32[1,8192]{1,0:T(1,128)S(1)}, u32[]{:S(2)}, u32[]{:S(2)}) collective-permute-start(f32[1,8192]{1,0:T(1,128)S(1)} %get-tuple-element.51), channel_id=1, source_target_pairs={{16,0},{32,16},{48,32},{64,48},{80,64},{96,80},{112,96},{128,112},... | collective-permute-start | bytes 98312 | tf_op jit(solution)/shard_map/ppermute | solution.py:22
  120.4 1.5 copy-start.5
  121.9 9.2 %collective-permute-start.12 = (f32[16,1,512]{2,1,0:T(1,128)S(1)}, f32[16,1,512]{2,1,0:T(1,128)S(1)}, u32[]{:S(2)}, u32[]{:S(2)}) collective-permute-start(f32[16,1,512]{2,1,0:T(1,128)S(1)} %get-tuple-element.48), channel_id=1, source_target_pairs={{16,0},{32,16},{48,32},{64,48},{80,64},{96,80},{112,96},{128,112},... | collective-permute-start | bytes 98312 | tf_op jit(solution)/shard_map/ppermute | solution.py:22
  129.2 8.9 %collective-permute-start.13 = (f32[16,1,512]{2,1,0:T(1,128)S(1)}, f32[16,1,512]{2,1,0:T(1,128)S(1)}, u32[]{:S(2)}, u32[]{:S(2)}) collective-permute-start(f32[16,1,512]{2,1,0:T(1,128)S(1)} %get-tuple-element.47), channel_id=1, source_target_pairs={{0,16},{16,32},{32,48},{48,64},{64,80},{80,96},{96,112},{112,128},... | collective-permute-start | bytes 98312 | tf_op jit(solution)/shard_map/ppermute | solution.py:20
  138.3 7.0 %collective-permute-start.14 = (f32[16,18,1]{2,1,0:T(8,128)S(1)}, f32[16,18,1]{2,1,0:T(8,128)S(1)}, u32[]{:S(2)}, u32[]{:S(2)}) collective-permute-start(f32[16,18,1]{2,1,0:T(8,128)S(1)} %get-tuple-element.43), channel_id=1, source_target_pairs={{1,0},{2,1},{3,2},{4,3},{5,4},{6,5},{7,6},{8,7},{9,8},{10,9},{11,1... | collective-permute-start | bytes 3464 | tf_op jit(solution)/shard_map/ppermute | solution.py:22
  140.2 9.3 %collective-permute-start.15 = (f32[16,18,1]{2,1,0:T(8,128)S(1)}, f32[16,18,1]{2,1,0:T(8,128)S(1)}, u32[]{:S(2)}, u32[]{:S(2)}) collective-permute-start(f32[16,18,1]{2,1,0:T(8,128)S(1)} %get-tuple-element.44), channel_id=1, source_target_pairs={{0,1},{1,2},{2,3},{3,4},{4,5},{5,6},{6,7},{7,8},{8,9},{9,10},{10,1... | collective-permute-start | bytes 3464 | tf_op jit(solution)/shard_map/ppermute | solution.py:20
  (1 other events, 1.0 us)
where the time goes:
time: 152 us
  starting transfers between devices  66.2 us (44%)
  blocking collectives  41.6 us (27%)
  waiting for transfers between devices  22.3 us (15%)
  other arithmetic  17.7 us (12%)
  local copies, waits for them, and re-layouts  2.78 us (2%)
    all_gather x1, blocking collectives, body(): top_rows = lax.all_gather(top, ('gy', 'ga'), axis=1, tiled=True)  41.6 us
    ppermute x8, starting transfers between devices, with_halo(): lax.ppermute(head, axis, [((i + 1) % count, i) for i in range(ends)])  36 us
    ppermute x8, starting transfers between devices, with_halo(): lax.ppermute(tail, axis, [(i, (i + 1) % count) for i in range(ends)])  30.2 us
    ppermute x8, waiting for transfers between devices, with_halo(): lax.ppermute(tail, axis, [(i, (i + 1) % count) for i in range(ends)])  11.2 us
    ppermute x8, waiting for transfers between devices, with_halo(): lax.ppermute(head, axis, [((i + 1) % count, i) for i in range(ends)])  11.1 us
    select_n x6, other arithmetic, guarded(): return jnp.where(denom > 0, numer / jnp.where(denom > 0, denom, 1.0), 0.0)  7.39 us
    concatenate x2, other arithmetic, with_halo(): jnp.concatenate([lax.ppermute(tail, axis, [(i, (i + 1) % count) for i in...  4.3 us
  transfers between devices with their start and end apart: 16, of which 7 were waited for; matrix products, arithmetic and copies ran while one was open for 2% of the time, Pallas kernels for 0%

commit v1 on v0

--- a/solution.py
+++ b/solution.py
@@ -84,7 +84,9 @@
     coupling_rows = exchange_coef * land_mask.astype(jnp.float32)
     coupling = lax.dynamic_slice_in_dim(coupling_rows, offset, cols_here, 1)
     top = head[0]
-    top_rows = lax.all_gather(top, ("gy", "ga"), axis=1, tiled=True)
+    top_rows = jnp.concatenate(
+        lax.all_to_all(jnp.stack([top] * lax.axis_size(("gy", "ga"))), ("gy", "ga"), 0, 0), axis=1
+    )
     drag = conveyance * jnp.power(depth, 5.0 / 3.0)
     sbase = depth + coupling_rows * top_rows
     sdiag = 1.0 + coupling_rows

time: 152 us -> 137 us (0.901)
  the two profiles are of different devices: /device:TPU:34 before, /device:TPU:47 now
where the time goes in v1:
time: 137 us; the launch traced here: 136 us
  starting transfers between devices  75.1 us (55%)
  waiting for transfers between devices  32.9 us (24%)
  other arithmetic  20.1 us (15%)
  local copies, waits for them, and re-layouts  6.75 us (5%)
    ppermute x8, starting transfers between devices, with_halo(): lax.ppermute(head, axis, [((i + 1) % count, i) for i in range(ends)])  35.1 us
    ppermute x8, starting transfers between devices, with_halo(): lax.ppermute(tail, axis, [(i, (i + 1) % count) for i in range(ends)])  33.6 us
    ppermute x8, waiting for transfers between devices, with_halo(): lax.ppermute(head, axis, [((i + 1) % count, i) for i in range(ends)])  17.8 us
    ppermute x8, waiting for transfers between devices, with_halo(): lax.ppermute(tail, axis, [(i, (i + 1) % count) for i in range(ends)])  15.1 us
    select_n x6, other arithmetic, guarded(): return jnp.where(denom > 0, numer / jnp.where(denom > 0, denom, 1.0), 0.0)  9.99 us
    all_to_all x1, starting transfers between devices, body(): lax.all_to_all(jnp.stack([top] * lax.axis_size(('gy', 'ga'))), ('gy', 'ga...  6.39 us
    concatenate x2, other arithmetic, with_halo(): jnp.concatenate([lax.ppermute(tail, axis, [(i, (i + 1) % count) for i in...  3.15 us
  transfers between devices with their start and end apart: 17, of which 9 were waited for; matrix products, arithmetic and copies ran while one was open for 7% of the time, Pallas kernels for 0%

profile of v1, /device:TPU:47, one launch (start us, length us, event | category | flops | bytes accessed | tf_op | source)
XLA Modules:
  0.0 136.0 jit_solution(1927663944034928425)
XLA Ops:
  4.3 4.9 %collective-permute-start.4 = (f32[3,1,8192]{2,1,0:T(1,128)S(1)}, f32[3,1,8192]{2,1,0:T(1,128)S(1)}, u32[]{:S(2)}, u32[]{:S(2)}) collective-permute-start(f32[3,1,8192]{2,1,0:T(1,128)S(1)} %get-tuple-element.35), channel_id=1, source_target_pairs={{0,16},{16,32},{32,48},{48,64},{64,80},{80,96},{96,112},{112,128},... | collective-permute-start | bytes 294920 | tf_op jit(solution)/shard_map/ppermute | solution.py:20
  9.2 4.3 %collective-permute-start.5 = (f32[3,1,8192]{2,1,0:T(1,128)S(1)}, f32[3,1,8192]{2,1,0:T(1,128)}, u32[]{:S(2)}, u32[]{:S(2)}) collective-permute-start(f32[3,1,8192]{2,1,0:T(1,128)S(1)} %get-tuple-element.36), channel_id=1, source_target_pairs={{16,0},{32,16},{48,32},{64,48},{80,64},{96,80},{112,96},{128,112},... | collective-permute-start | bytes 294920 | tf_op jit(solution)/shard_map/ppermute | solution.py:22
  14.4 6.4 %all-to-all-start = ((f32[16,16,512]{2,1,0:T(8,128)}), f32[16,16,512]{2,1,0:T(8,128)}, u32[]{:S(2)}, u32[]{:S(2)}) async-start(f32[16,16,512]{2,1,0:T(8,128)} %stack.31), calls=%async_computation | async-start | bytes 1048576 | tf_op jit(solution)/shard_map/all_to_all | solution.py:88
  21.0 2.8 %collective-permute-start = (f32[2,16,1,512]{3,2,1,0:T(1,128)S(1)}, f32[2,16,1,512]{3,2,1,0:T(1,128)S(1)}, u32[]{:S(2)}, u32[]{:S(2)}) collective-permute-start(f32[2,16,1,512]{3,2,1,0:T(1,128)S(1)} %get-tuple-element.39), channel_id=1, source_target_pairs={{0,16},{16,32},{32,48},{48,64},{64,80},{80,96},{96,112},{112,128},... | collective-permute-start | bytes 196616 | tf_op jit(solution)/shard_map/ppermute | solution.py:20
  23.8 5.5 %collective-permute-start.1 = (f32[2,16,1,512]{3,2,1,0:T(1,128)S(1)}, f32[2,16,1,512]{3,2,1,0:T(1,128)S(1)}, u32[]{:S(2)}, u32[]{:S(2)}) collective-permute-start(f32[2,16,1,512]{3,2,1,0:T(1,128)S(1)} %get-tuple-element.40), channel_id=1, source_target_pairs={{16,0},{32,16},{48,32},{64,48},{80,64},{96,80},{112,96},{128,112},... | collective-permute-start | bytes 196616 | tf_op jit(solution)/shard_map/ppermute | solution.py:22
  31.5 5.9 %collective-permute-start.2 = (f32[2,16,18,1]{3,2,1,0:T(8,128)S(1)}, f32[2,16,18,1]{3,2,1,0:T(8,128)S(1)}, u32[]{:S(2)}, u32[]{:S(2)}) collective-permute-start(f32[2,16,18,1]{3,2,1,0:T(8,128)S(1)} %get-tuple-element.37), channel_id=1, source_target_pairs={{0,1},{1,2},{2,3},{3,4},{4,5},{5,6},{6,7},{7,8},{8,9},{9,10},{10,1... | collective-permute-start | bytes 6920 | tf_op jit(solution)/shard_map/ppermute | solution.py:20
  40.3 6.1 %collective-permute-done.2 = f32[2,16,18,1]{3,2,1,0:T(8,128)S(1)} collective-permute-done((f32[2,16,18,1]{3,2,1,0:T(8,128)S(1)}, f32[2,16,18,1]{3,2,1,0:T(8,128)S(1)}, u32[]{:S(2)}, u32[]{:S(2)}) %collective-permute-start.2) | collective-permute-done | bytes 2336 | tf_op jit(solution)/shard_map/ppermute | solution.py:20
  46.4 7.5 %collective-permute-done.3 = f32[2,16,18,1]{3,2,1,0:T(8,128)S(1)} collective-permute-done((f32[2,16,18,1]{3,2,1,0:T(8,128)S(1)}, f32[2,16,18,1]{3,2,1,0:T(8,128)S(1)}, u32[]{:S(2)}, u32[]{:S(2)}) %collective-permute-start.3) | collective-permute-done | bytes 2336 | tf_op jit(solution)/shard_map/ppermute | solution.py:22
  56.8 2.0 %select_maximum_fusion = f32[3,18,8194]{2,1,0:T(8,128)S(1)} fusion(f32[3,1,8192]{2,1,0:T(1,128)} %collective-permute-done.5, f32[3,1,8192]{2,1,0:T(1,128)S(1)} %collective-permute-done.4, f32[1,16,8192]{2,1,0:T(8,128)S(1)} %bitcast.48, f32[1,16,8192]{2,1,0:T(8,128)S(1)} %copy-done.9, f32[1,16,8192]{2,1,0:T(8,128)S(1)} %bitcast.36), kind=kLoop, calls=%fused_computation.2 | loop fusion | flops 5309712 | bytes 3539376 | tf_op jit(solution)/shard_map/concatenate | solution.py:18
  62.3 3.9 %fusion.59 = (f32[16,8192]{1,0:T(8,128)S(1)}, f32[16,8192]{1,0:T(8,128)S(1)}, f32[16,8192]{1,0:T(8,128)S(1)}, f32[16,8192]{1,0:T(8,128)S(1)}, f32[16,8192]{1,0:T(8,128)S(1)}, /*index=5*/f32[16,8192]{1,0:T(8,128)S(1)}) fusion(f32[18,8194]{1,0:T(8,128)} %fusion.4, f32[18,8194]{1,0:T(8,128)} %get-tuple-element.32, s32[16,8192]{1,0:T(8,128)} %param.21, ...), kind=kLoop, calls=%fused_computation.116 | loop fusion | flops 5767168 | bytes 9961472 | tf_op jit(solution)/shard_map/jit(_where)/select_n | solution.py:51
  66.3 6.1 %collective-permute-start.6 = (f32[1,8192]{1,0:T(1,128)S(1)}, f32[1,8192]{1,0:T(1,128)S(1)}, u32[]{:S(2)}, u32[]{:S(2)}) collective-permute-start(f32[1,8192]{1,0:T(1,128)S(1)} %get-tuple-element.54), channel_id=1, source_target_pairs={{0,16},{16,32},{32,48},{48,64},{64,80},{80,96},{96,112},{112,128},... | collective-permute-start | bytes 98312 | tf_op jit(solution)/shard_map/ppermute | solution.py:20
  72.3 2.3 %collective-permute-start.7 = (f32[1,8192]{1,0:T(1,128)S(1)}, f32[1,8192]{1,0:T(1,128)S(1)}, u32[]{:S(2)}, u32[]{:S(2)}) collective-permute-start(f32[1,8192]{1,0:T(1,128)S(1)} %get-tuple-element.55), channel_id=1, source_target_pairs={{16,0},{32,16},{48,32},{64,48},{80,64},{96,80},{112,96},{128,112},... | collective-permute-start | bytes 98312 | tf_op jit(solution)/shard_map/ppermute | solution.py:22
  75.0 3.6 %collective-permute-done.7 = f32[1,8192]{1,0:T(1,128)S(1)} collective-permute-done((f32[1,8192]{1,0:T(1,128)S(1)}, f32[1,8192]{1,0:T(1,128)S(1)}, u32[]{:S(2)}, u32[]{:S(2)}) %collective-permute-start.7) | collective-permute-done | bytes 32800 | tf_op jit(solution)/shard_map/ppermute | solution.py:22
  79.9 2.4 %collective-permute-start.8 = (f32[1,8192]{1,0:T(1,128)S(1)}, f32[1,8192]{1,0:T(1,128)S(1)}, u32[]{:S(2)}, u32[]{:S(2)}) collective-permute-start(f32[1,8192]{1,0:T(1,128)S(1)} %get-tuple-element.52), channel_id=1, source_target_pairs={{0,16},{16,32},{32,48},{48,64},{64,80},{80,96},{96,112},{112,128},... | collective-permute-start | bytes 98312 | tf_op jit(solution)/shard_map/ppermute | solution.py:20
  82.4 5.9 %collective-permute-start.9 = (f32[1,8192]{1,0:T(1,128)S(1)}, f32[1,8192]{1,0:T(1,128)S(1)}, u32[]{:S(2)}, u32[]{:S(2)}) collective-permute-start(f32[1,8192]{1,0:T(1,128)S(1)} %get-tuple-element.53), channel_id=1, source_target_pairs={{16,0},{32,16},{48,32},{64,48},{80,64},{96,80},{112,96},{128,112},... | collective-permute-start | bytes 98312 | tf_op jit(solution)/shard_map/ppermute | solution.py:22
  90.5 2.4 %collective-permute-start.10 = (f32[1,8192]{1,0:T(1,128)S(1)}, f32[1,8192]{1,0:T(1,128)S(1)}, u32[]{:S(2)}, u32[]{:S(2)}) collective-permute-start(f32[1,8192]{1,0:T(1,128)S(1)} %get-tuple-element.50), channel_id=1, source_target_pairs={{0,16},{16,32},{32,48},{48,64},{64,80},{80,96},{96,112},{112,128},... | collective-permute-start | bytes 98312 | tf_op jit(solution)/shard_map/ppermute | solution.py:20
  92.9 6.6 %collective-permute-start.11 = (f32[1,8192]{1,0:T(1,128)S(1)}, f32[1,8192]{1,0:T(1,128)S(1)}, u32[]{:S(2)}, u32[]{:S(2)}) collective-permute-start(f32[1,8192]{1,0:T(1,128)S(1)} %get-tuple-element.51), channel_id=1, source_target_pairs={{16,0},{32,16},{48,32},{64,48},{80,64},{96,80},{112,96},{128,112},... | collective-permute-start | bytes 98312 | tf_op jit(solution)/shard_map/ppermute | solution.py:22
  103.4 6.7 %collective-permute-start.12 = (f32[16,1,512]{2,1,0:T(1,128)S(1)}, f32[16,1,512]{2,1,0:T(1,128)S(1)}, u32[]{:S(2)}, u32[]{:S(2)}) collective-permute-start(f32[16,1,512]{2,1,0:T(1,128)S(1)} %get-tuple-element.48), channel_id=1, source_target_pairs={{16,0},{32,16},{48,32},{64,48},{80,64},{96,80},{112,96},{128,112},... | collective-permute-start | bytes 98312 | tf_op jit(solution)/shard_map/ppermute | solution.py:22
  110.0 1.9 %collective-permute-start.13 = (f32[16,1,512]{2,1,0:T(1,128)S(1)}, f32[16,1,512]{2,1,0:T(1,128)S(1)}, u32[]{:S(2)}, u32[]{:S(2)}) collective-permute-start(f32[16,1,512]{2,1,0:T(1,128)S(1)} %get-tuple-element.47), channel_id=1, source_target_pairs={{0,16},{16,32},{32,48},{48,64},{64,80},{80,96},{96,112},{112,128},... | collective-permute-start | bytes 98312 | tf_op jit(solution)/shard_map/ppermute | solution.py:20
  112.0 5.7 %collective-permute-done.13 = f32[16,1,512]{2,1,0:T(1,128)S(1)} collective-permute-done((f32[16,1,512]{2,1,0:T(1,128)S(1)}, f32[16,1,512]{2,1,0:T(1,128)S(1)}, u32[]{:S(2)}, u32[]{:S(2)}) %collective-permute-start.13) | collective-permute-done | bytes 32800 | tf_op jit(solution)/shard_map/ppermute | solution.py:20
  119.8 7.1 %collective-permute-start.15 = (f32[16,18,1]{2,1,0:T(8,128)S(1)}, f32[16,18,1]{2,1,0:T(8,128)S(1)}, u32[]{:S(2)}, u32[]{:S(2)}) collective-permute-start(f32[16,18,1]{2,1,0:T(8,128)S(1)} %get-tuple-element.44), channel_id=1, source_target_pairs={{0,1},{1,2},{2,3},{3,4},{4,5},{5,6},{6,7},{7,8},{8,9},{9,10},{10,1... | collective-permute-start | bytes 3464 | tf_op jit(solution)/shard_map/ppermute | solution.py:20
  127.1 3.4 %collective-permute-done.14 = f32[16,18,1]{2,1,0:T(8,128)S(1)} collective-permute-done((f32[16,18,1]{2,1,0:T(8,128)S(1)}, f32[16,18,1]{2,1,0:T(8,128)S(1)}, u32[]{:S(2)}, u32[]{:S(2)}) %collective-permute-start.14) | collective-permute-done | bytes 1184 | tf_op jit(solution)/shard_map/ppermute | solution.py:22
  130.4 3.3 %collective-permute-done.15 = f32[16,18,1]{2,1,0:T(8,128)S(1)} collective-permute-done((f32[16,18,1]{2,1,0:T(8,128)S(1)}, f32[16,18,1]{2,1,0:T(8,128)S(1)}, u32[]{:S(2)}, u32[]{:S(2)}) %collective-permute-start.15) | collective-permute-done | bytes 1184 | tf_op jit(solution)/shard_map/ppermute | solution.py:20
  133.7 2.3 %fusion.20 = f32[16,16,512]{2,1,0:T(8,128)} fusion(f32[16,16,512]{2,1,0:T(8,128)S(1)} %fusion.63, f32[16,18,1]{2,1,0:T(8,128)S(1)} %collective-permute-done.15, f32[16,1,512]{2,1,0:T(1,128)S(1)} %collective-permute-done.12, f32[16,16,512]{2,1,0:T(8,128)S(1)} %fusion.31, f32[16,1,512]{2,1,0:T(1,128)S(1)} %collective-permute-done.13, ...), kind=kLoop, calls=%fused_computation.52 | loop fusion | flops 6946816 | bytes 5769472 | tf_op jit(solution)/shard_map/jit(_where)/select_n | solution.py:51
  (76 shorter events, 25.9 us)
Async XLA Ops:
  0.6 12.9 %copy-start.5 = (f32[16,16,512]{2,1,0:T(8,128)S(1)}, f32[16,16,512]{2,1,0:T(8,128)}, u32[]{:S(2)}) copy-start(f32[16,16,512]{2,1,0:T(8,128)} %param.13) | copy-start | bytes 1572868
  0.6 20.2 %copy-start.10 = (f32[16,16,512]{2,1,0:T(8,128)S(1)}, f32[16,16,512]{2,1,0:T(8,128)}, u32[]{:S(2)}) copy-start(f32[16,16,512]{2,1,0:T(8,128)} %param.14) | copy-start | bytes 1572868
  2.2 27.0 %copy-start.13 = (s32[16,512]{1,0:T(8,128)S(1)}, s32[16,512]{1,0:T(8,128)}, u32[]{:S(2)}) copy-start(s32[16,512]{1,0:T(8,128)} %param.15) | copy-start | bytes 98308
  2.2 27.1 %copy-start.14 = (s32[16,512]{1,0:T(8,128)S(1)}, s32[16,512]{1,0:T(8,128)}, u32[]{:S(2)}) copy-start(s32[16,512]{1,0:T(8,128)} %param.16) | copy-start | bytes 98308
  2.2 27.1 %copy-start.15 = (f32[17]{0:T(128)S(1)}, f32[17]{0:T(128)}, u32[]{:S(2)}) copy-start(f32[17]{0:T(128)} %param.17) | copy-start | bytes 208
  4.3 51.9 %collective-permute-start.4 = (f32[3,1,8192]{2,1,0:T(1,128)S(1)}, f32[3,1,8192]{2,1,0:T(1,128)S(1)}, u32[]{:S(2)}, u32[]{:S(2)}) collective-permute-start(f32[3,1,8192]{2,1,0:T(1,128)S(1)} %get-tuple-element.35), channel_id=1, source_target_pairs={{0,16},{16,32},{32,48},{48,64},{64,80},{80,96},{96,112},{112,128},... | collective-permute-start | bytes 294920 | tf_op jit(solution)/shard_map/ppermute | solution.py:20
  9.2 46.9 %collective-permute-start.5 = (f32[3,1,8192]{2,1,0:T(1,128)S(1)}, f32[3,1,8192]{2,1,0:T(1,128)}, u32[]{:S(2)}, u32[]{:S(2)}) collective-permute-start(f32[3,1,8192]{2,1,0:T(1,128)S(1)} %get-tuple-element.36), channel_id=1, source_target_pairs={{16,0},{32,16},{48,32},{64,48},{80,64},{96,80},{112,96},{128,112},... | collective-permute-start | bytes 294920 | tf_op jit(solution)/shard_map/ppermute | solution.py:22
  14.4 46.6 %all-to-all-start = ((f32[16,16,512]{2,1,0:T(8,128)}), f32[16,16,512]{2,1,0:T(8,128)}, u32[]{:S(2)}, u32[]{:S(2)}) async-start(f32[16,16,512]{2,1,0:T(8,128)} %stack.31), calls=%async_computation | async-start | bytes 1048576 | tf_op jit(solution)/shard_map/all_to_all | solution.py:88
  21.0 8.5 %collective-permute-start = (f32[2,16,1,512]{3,2,1,0:T(1,128)S(1)}, f32[2,16,1,512]{3,2,1,0:T(1,128)S(1)}, u32[]{:S(2)}, u32[]{:S(2)}) collective-permute-start(f32[2,16,1,512]{3,2,1,0:T(1,128)S(1)} %get-tuple-element.39), channel_id=1, source_target_pairs={{0,16},{16,32},{32,48},{48,64},{64,80},{80,96},{96,112},{112,128},... | collective-permute-start | bytes 196616 | tf_op jit(solution)/shard_map/ppermute | solution.py:20
  23.8 7.5 %collective-permute-start.1 = (f32[2,16,1,512]{3,2,1,0:T(1,128)S(1)}, f32[2,16,1,512]{3,2,1,0:T(1,128)S(1)}, u32[]{:S(2)}, u32[]{:S(2)}) collective-permute-start(f32[2,16,1,512]{3,2,1,0:T(1,128)S(1)} %get-tuple-element.40), channel_id=1, source_target_pairs={{16,0},{32,16},{48,32},{64,48},{80,64},{96,80},{112,96},{128,112},... | collective-permute-start | bytes 196616 | tf_op jit(solution)/shard_map/ppermute | solution.py:22
  31.5 14.8 %collective-permute-start.2 = (f32[2,16,18,1]{3,2,1,0:T(8,128)S(1)}, f32[2,16,18,1]{3,2,1,0:T(8,128)S(1)}, u32[]{:S(2)}, u32[]{:S(2)}) collective-permute-start(f32[2,16,18,1]{3,2,1,0:T(8,128)S(1)} %get-tuple-element.37), channel_id=1, source_target_pairs={{0,1},{1,2},{2,3},{3,4},{4,5},{5,6},{6,7},{7,8},{8,9},{9,10},{10,1... | collective-permute-start | bytes 6920 | tf_op jit(solution)/shard_map/ppermute | solution.py:20
  37.5 16.4 %collective-permute-start.3 = (f32[2,16,18,1]{3,2,1,0:T(8,128)S(1)}, f32[2,16,18,1]{3,2,1,0:T(8,128)S(1)}, u32[]{:S(2)}, u32[]{:S(2)}) collective-permute-start(f32[2,16,18,1]{3,2,1,0:T(8,128)S(1)} %get-tuple-element.38), channel_id=1, source_target_pairs={{1,0},{2,1},{3,2},{4,3},{5,4},{6,5},{7,6},{8,7},{9,8},{10,9},{11,1... | collective-permute-start | bytes 6920 | tf_op jit(solution)/shard_map/ppermute | solution.py:22
  66.2 12.9 %copy-start.1 = (f32[16,8192]{1,0:T(8,128)S(1)}, f32[16,8192]{1,0:T(8,128)}, u32[]{:S(2)}) copy-start(f32[16,8192]{1,0:T(8,128)} %param.18) | copy-start | bytes 1572868
  66.2 12.9 %copy-start.4 = (f32[18,8194]{1,0:T(8,128)S(1)}, f32[18,8194]{1,0:T(8,128)}, u32[]{:S(2)}) copy-start(f32[18,8194]{1,0:T(8,128)} %get-tuple-element.32) | copy-start | bytes 1769908
  66.3 8.8 %collective-permute-start.6 = (f32[1,8192]{1,0:T(1,128)S(1)}, f32[1,8192]{1,0:T(1,128)S(1)}, u32[]{:S(2)}, u32[]{:S(2)}) collective-permute-start(f32[1,8192]{1,0:T(1,128)S(1)} %get-tuple-element.54), channel_id=1, source_target_pairs={{0,16},{16,32},{32,48},{48,64},{64,80},{80,96},{96,112},{112,128},... | collective-permute-start | bytes 98312 | tf_op jit(solution)/shard_map/ppermute | solution.py:20
  72.3 6.3 %collective-permute-start.7 = (f32[1,8192]{1,0:T(1,128)S(1)}, f32[1,8192]{1,0:T(1,128)S(1)}, u32[]{:S(2)}, u32[]{:S(2)}) collective-permute-start(f32[1,8192]{1,0:T(1,128)S(1)} %get-tuple-element.55), channel_id=1, source_target_pairs={{16,0},{32,16},{48,32},{64,48},{80,64},{96,80},{112,96},{128,112},... | collective-permute-start | bytes 98312 | tf_op jit(solution)/shard_map/ppermute | solution.py:22
  79.9 8.6 %collective-permute-start.8 = (f32[1,8192]{1,0:T(1,128)S(1)}, f32[1,8192]{1,0:T(1,128)S(1)}, u32[]{:S(2)}, u32[]{:S(2)}) collective-permute-start(f32[1,8192]{1,0:T(1,128)S(1)} %get-tuple-element.52), channel_id=1, source_target_pairs={{0,16},{16,32},{32,48},{48,64},{64,80},{80,96},{96,112},{112,128},... | collective-permute-start | bytes 98312 | tf_op jit(solution)/shard_map/ppermute | solution.py:20
  82.4 6.9 %collective-permute-start.9 = (f32[1,8192]{1,0:T(1,128)S(1)}, f32[1,8192]{1,0:T(1,128)S(1)}, u32[]{:S(2)}, u32[]{:S(2)}) collective-permute-start(f32[1,8192]{1,0:T(1,128)S(1)} %get-tuple-element.53), channel_id=1, source_target_pairs={{16,0},{32,16},{48,32},{64,48},{80,64},{96,80},{112,96},{128,112},... | collective-permute-start | bytes 98312 | tf_op jit(solution)/shard_map/ppermute | solution.py:22
  90.5 9.1 %collective-permute-start.10 = (f32[1,8192]{1,0:T(1,128)S(1)}, f32[1,8192]{1,0:T(1,128)S(1)}, u32[]{:S(2)}, u32[]{:S(2)}) collective-permute-start(f32[1,8192]{1,0:T(1,128)S(1)} %get-tuple-element.50), channel_id=1, source_target_pairs={{0,16},{16,32},{32,48},{48,64},{64,80},{80,96},{96,112},{112,128},... | collective-permute-start | bytes 98312 | tf_op jit(solution)/shard_map/ppermute | solution.py:20
  92.9 7.4 %collective-permute-start.11 = (f32[1,8192]{1,0:T(1,128)S(1)}, f32[1,8192]{1,0:T(1,128)S(1)}, u32[]{:S(2)}, u32[]{:S(2)}) collective-permute-start(f32[1,8192]{1,0:T(1,128)S(1)} %get-tuple-element.51), channel_id=1, source_target_pairs={{16,0},{32,16},{48,32},{64,48},{80,64},{96,80},{112,96},{128,112},... | collective-permute-start | bytes 98312 | tf_op jit(solution)/shard_map/ppermute | solution.py:22
  103.4 8.6 %collective-permute-start.12 = (f32[16,1,512]{2,1,0:T(1,128)S(1)}, f32[16,1,512]{2,1,0:T(1,128)S(1)}, u32[]{:S(2)}, u32[]{:S(2)}) collective-permute-start(f32[16,1,512]{2,1,0:T(1,128)S(1)} %get-tuple-element.48), channel_id=1, source_target_pairs={{16,0},{32,16},{48,32},{64,48},{80,64},{96,80},{112,96},{128,112},... | collective-permute-start | bytes 98312 | tf_op jit(solution)/shard_map/ppermute | solution.py:22
  110.0 7.7 %collective-permute-start.13 = (f32[16,1,512]{2,1,0:T(1,128)S(1)}, f32[16,1,512]{2,1,0:T(1,128)S(1)}, u32[]{:S(2)}, u32[]{:S(2)}) collective-permute-start(f32[16,1,512]{2,1,0:T(1,128)S(1)} %get-tuple-element.47), channel_id=1, source_target_pairs={{0,16},{16,32},{32,48},{48,64},{64,80},{80,96},{96,112},{112,128},... | collective-permute-start | bytes 98312 | tf_op jit(solution)/shard_map/ppermute | solution.py:20
  117.9 12.6 %collective-permute-start.14 = (f32[16,18,1]{2,1,0:T(8,128)S(1)}, f32[16,18,1]{2,1,0:T(8,128)S(1)}, u32[]{:S(2)}, u32[]{:S(2)}) collective-permute-start(f32[16,18,1]{2,1,0:T(8,128)S(1)} %get-tuple-element.43), channel_id=1, source_target_pairs={{1,0},{2,1},{3,2},{4,3},{5,4},{6,5},{7,6},{8,7},{9,8},{10,9},{11,1... | collective-permute-start | bytes 3464 | tf_op jit(solution)/shard_map/ppermute | solution.py:22
  119.8 13.9 %collective-permute-start.15 = (f32[16,18,1]{2,1,0:T(8,128)S(1)}, f32[16,18,1]{2,1,0:T(8,128)S(1)}, u32[]{:S(2)}, u32[]{:S(2)}) collective-permute-start(f32[16,18,1]{2,1,0:T(8,128)S(1)} %get-tuple-element.44), channel_id=1, source_target_pairs={{0,1},{1,2},{2,3},{3,4},{4,5},{5,6},{6,7},{7,8},{8,9},{9,10},{10,1... | collective-permute-start | bytes 3464 | tf_op jit(solution)/shard_map/ppermute | solution.py:20
  (9 other events, 34.2 us)
